TPU v7x, 32 devices: a whole 2x2x4 slice. The times are simulated.
32 devices in a mesh: groups: 2 (over y), srv: 4 (over z), hid: 2 (over x), rep: 2 (over core).
Axes of the slice: x: 2, y: 2, z: 4, core: 2. Of those that a mesh axis runs over, the one named last changes fastest.
Arguments:
- layer_input: bfloat16 [2048, 4096], P(('groups', 'srv'), ('hid', 'rep')), parts along dimension 0, may hold values from -12 to 12
- query_weight: bfloat16 [4096, 4096], P('srv', ('hid', 'rep')), may hold values from -0.09375 to 0.09375
- key_weight: bfloat16 [4096, 1024], P('srv', ('hid', 'rep')), may hold values from -0.09375 to 0.09375
- value_weight: bfloat16 [4096, 1024], P('srv', ('hid', 'rep')), may hold values from -0.09375 to 0.09375
- out_grad: bfloat16 [2048, 4096], P(('groups', 'srv'), ('hid', 'rep')), parts along dimension 0, may hold values from -6 to 6
- doc_ids: int32 [2048], P('groups'), parts along dimension 0, may hold values from 0 to 7, never falling along the last dimension, each value on 1 to 512 neighbouring positions
Outputs:
- input_grad: bfloat16 [2048, 4096], P(('groups', 'srv'), ('hid', 'rep')), parts along dimension 0
- query_weight_grad: float32 [8192, 4096], P(('groups', 'srv'), ('hid', 'rep')), parts along dimension 0
- key_weight_grad: float32 [8192, 1024], P(('groups', 'srv'), ('hid', 'rep')), parts along dimension 0
- value_weight_grad: float32 [8192, 1024], P(('groups', 'srv'), ('hid', 'rep')), parts along dimension 0
There are 2 independent parts, one for each index of `groups`. A program takes and returns all parts, laid end to end along the dimension named above; an argument that names none is the same for every part. Nothing has to cross between parts.
Inputs may be any that keep to these rules, and one draw needn't show every extreme that they name: `doc_ids`: document numbers never fall along the tokens; every document holds at most 512 tokens and one holds exactly 512.
All inputs are finite; a program needn't handle non-finite values.
Results may differ from a plain program's by a relative error of at most 0.011.
Values may be sent and summed in bfloat16 or wider, within the bound.
A program may use at most 64 MiB of HBM per device.

v0:
```python
import jax
import jax.numpy as jnp
from jax import lax
from jax.sharding import PartitionSpec as P

HQ = 32
HK = 8
DH = 128
BLOCK = 128


NEGATIVE = -1e30


def attend(queries, cotangent, keys_all, values_all, doc_ids, block_id, carried):
    row_count = queries.shape[0]
    factor_scale = queries.shape[-1] ** (-0.5)
    offsets = jnp.arange(row_count, dtype=jnp.int32)
    query_pos = block_id * row_count + offsets
    query_doc = lax.dynamic_slice_in_dim(doc_ids, block_id * row_count, row_count)
    doc_start = jnp.sum((doc_ids < query_doc[0]).astype(jnp.int32))
    lowest = doc_start // row_count
    highest = jnp.where(True, block_id + 1, lowest)

    def scores_at(key_block):
        key_rows = lax.dynamic_slice_in_dim(keys_all, key_block * row_count, row_count, 0)
        value_rows = lax.dynamic_slice_in_dim(values_all, key_block * row_count, row_count, 0)
        key_doc = lax.dynamic_slice_in_dim(doc_ids, key_block * row_count, row_count)
        key_pos = key_block * row_count + offsets
        allowed = (key_doc[None, :] == query_doc[:, None]) & (
            key_pos[None, :] <= query_pos[:, None]
        )
        logits = (
            jnp.einsum("qgnd,kgd->gnqk", queries, key_rows, preferred_element_type=jnp.float32)
            * factor_scale
        )
        logits = jnp.where(allowed, logits, NEGATIVE)
        slopes = jnp.einsum(
            "qgnd,kgd->gnqk", cotangent, value_rows, preferred_element_type=jnp.float32
        )
        return (key_rows, allowed, logits, slopes)

    def first_pass(key_block, loop_state):
        row_peak, row_total, row_inner = loop_state
        key_rows, allowed, logits, slopes = scores_at(key_block)
        new_peak = jnp.maximum(row_peak, jnp.max(logits, axis=-1))
        weights = jnp.where(allowed, jnp.exp(logits - new_peak[..., None]), 0.0)
        factor = jnp.exp(row_peak - new_peak)
        row_total = row_total * factor + jnp.sum(weights, axis=-1)
        row_inner = row_inner * factor + jnp.sum(weights * slopes, axis=-1)
        return (new_peak, row_total, row_inner)

    stat_shape = (queries.shape[1], queries.shape[2], row_count)
    initial = (
        jnp.full(stat_shape, NEGATIVE, jnp.float32),
        jnp.zeros(stat_shape, jnp.float32),
        jnp.zeros(stat_shape, jnp.float32),
    )
    row_peak, row_total, row_inner = lax.fori_loop(lowest, highest, first_pass, initial)
    safe_total = jnp.where(True, row_total, 1.0)
    row_delta = row_inner / safe_total
    log_total = row_peak + jnp.log(safe_total)

    def second_pass(key_block, loop_state):
        query_grad, key_accum, value_accum = loop_state
        key_rows, allowed, logits, slopes = scores_at(key_block)
        attention = jnp.where(allowed, jnp.exp(logits - log_total[..., None]), 0.0)
        score_grad = (attention * (slopes - row_delta[..., None]) * factor_scale).astype(
            jnp.bfloat16
        )
        value_part = jnp.einsum(
            "gnqk,qgnd->kgd",
            attention.astype(jnp.bfloat16),
            cotangent,
            preferred_element_type=jnp.float32,
        )
        key_part = jnp.einsum(
            "gnqk,qgnd->kgd", score_grad, queries, preferred_element_type=jnp.float32
        )
        query_grad = query_grad + jnp.einsum(
            "gnqk,kgd->qgnd", score_grad, key_rows, preferred_element_type=jnp.float32
        )
        first_row = key_block * row_count
        key_accum = lax.dynamic_update_slice_in_dim(
            key_accum,
            lax.dynamic_slice_in_dim(key_accum, first_row, row_count, 0) + key_part,
            first_row,
            0,
        )
        value_accum = lax.dynamic_update_slice_in_dim(
            value_accum,
            lax.dynamic_slice_in_dim(value_accum, first_row, row_count, 0) + value_part,
            first_row,
            0,
        )
        return (query_grad, key_accum, value_accum)

    start_grad = jnp.zeros(queries.shape, jnp.float32)
    query_grad, key_accum, value_accum = lax.fori_loop(
        lowest, highest, second_pass, (start_grad, carried[0], carried[1])
    )
    return (query_grad, (key_accum, value_accum))


def body(layer_input, query_weight, key_weight, value_weight, out_grad, doc_ids):
    tok_rows = layer_input.shape[0]
    query_width = query_weight.shape[1]
    pair_width = key_weight.shape[1]
    key_heads = pair_width // DH
    group_size = HQ // HK
    block_count = tok_rows // BLOCK
    owner_id = lax.axis_index("srv")
    weights_all = lax.all_gather(
        jnp.concatenate([query_weight, key_weight, value_weight], axis=1), "srv", axis=0, tiled=True
    )
    inputs_all = lax.all_gather(layer_input, ("hid", "rep"), axis=1, tiled=True)
    projected = jnp.dot(inputs_all, weights_all, preferred_element_type=jnp.float32).astype(
        jnp.bfloat16
    )
    queries = projected[:, :query_width].reshape(block_count, BLOCK, key_heads, group_size, DH)
    keys_local = projected[:, query_width : query_width + pair_width]
    values_local = projected[:, query_width + pair_width :]
    keys_all, values_all = (
        lax.all_gather(keys_local, "srv", axis=0, tiled=True),
        lax.all_gather(values_local, "srv", axis=0, tiled=True),
    )
    total_rows = keys_all.shape[0]
    keys_all = keys_all.reshape(total_rows, key_heads, DH)
    values_all = values_all.reshape(total_rows, key_heads, DH)
    cotangent = out_grad.reshape(block_count, BLOCK, key_heads, group_size, DH)
    empty_accum = jnp.zeros((total_rows, key_heads, DH), jnp.float32)

    def own_block(position, loop_state):
        answers, carried = loop_state
        grad_q, carried = attend(
            lax.dynamic_index_in_dim(queries, position, 0, keepdims=False),
            lax.dynamic_index_in_dim(cotangent, position, 0, keepdims=False),
            keys_all,
            values_all,
            doc_ids,
            owner_id * block_count + position,
            carried,
        )
        answers = lax.dynamic_update_index_in_dim(answers, grad_q.astype(jnp.bfloat16), position, 0)
        return (answers, carried)

    answers = jnp.zeros(queries.shape, jnp.bfloat16)
    answers, carried = lax.fori_loop(
        0, block_count, own_block, (answers, (empty_accum, empty_accum))
    )
    query_grad = answers.reshape(tok_rows, query_width)
    key_accum, value_accum = carried
    key_sum, value_sum = (
        lax.psum_scatter(key_accum, "srv", scatter_dimension=0, tiled=True),
        lax.psum_scatter(value_accum, "srv", scatter_dimension=0, tiled=True),
    )
    grads_all = jnp.concatenate(
        [
            query_grad,
            key_sum.astype(jnp.bfloat16).reshape(tok_rows, pair_width),
            value_sum.astype(jnp.bfloat16).reshape(tok_rows, pair_width),
        ],
        axis=1,
    )
    input_terms = lax.dot_general(
        grads_all, weights_all, (((1,), (1,)), ((), ())), preferred_element_type=jnp.float32
    )
    input_grad = lax.psum_scatter(
        input_terms, ("hid", "rep"), scatter_dimension=1, tiled=True
    ).astype(jnp.bfloat16)
    columns = lax.all_to_all(inputs_all, "srv", split_axis=1, concat_axis=0, tiled=True)
    weight_grad = lax.dot_general(
        columns,
        lax.all_gather(grads_all, "srv", axis=0, tiled=True),
        (((0,), (0,)), ((), ())),
        preferred_element_type=jnp.float32,
    )
    return (
        input_grad,
        weight_grad[:, :query_width],
        weight_grad[:, query_width : query_width + pair_width],
        weight_grad[:, query_width + pair_width :],
    )


def solution(mesh):
    in_specs = (
        P(("groups", "srv"), ("hid", "rep")),
        P("srv", ("hid", "rep")),
        P("srv", ("hid", "rep")),
        P("srv", ("hid", "rep")),
        P(("groups", "srv"), ("hid", "rep")),
        P("groups"),
    )
    out_specs = (
        P(("groups", "srv"), ("hid", "rep")),
        P(("groups", "srv"), ("hid", "rep")),
        P(("groups", "srv"), ("hid", "rep")),
        P(("groups", "srv"), ("hid", "rep")),
    )
    return jax.shard_map(body, mesh=mesh, in_specs=in_specs, out_specs=out_specs, check_vma=False)
```

profile of v0, /device:TPU:0, one launch (start us, length us, event | category | flops | bytes accessed | tf_op | source)
XLA Modules:
  0.0 566.1 jit_solution(9984030902238712507)
XLA Ops:
  7.2 2.0 copy.34
  9.3 3.2 pad_maximum_fusion
  12.6 0.9 copy-done.1
  13.5 1.2 reshape.48
  14.7 20.7 %all-gather.6.cloned.1.call-done = bf16[256,4096]{0,1:T(8,128)(2,1)} async-done(((bf16[256,1024]{0,1:T(8,128)(2,1)}), bf16[256,4096]{0,1:T(8,128)(2,1)}) %all-gather.6.cloned.1.call-update) | async-done | bytes 2097168 | tf_op jit(solution)/shard_map/all_gather | solution.py:116
  35.4 220.4 %all-gather.4.cloned.1.call-done = bf16[4096,1536]{1,0:T(8,128)(2,1)} async-done(((bf16[1024,1536]{1,0:T(8,128)(2,1)}), bf16[4096,1536]{1,0:T(8,128)(2,1)}) %all-gather.4.cloned.1.call-update) | async-done | bytes 12582928 | tf_op jit(solution)/shard_map/all_gather | solution.py:113
  255.8 8.7 %fusion.43 = bf16[256,1536]{0,1:T(8,128)(2,1)S(1)} fusion(bf16[4096,1536]{1,0:T(8,128)(2,1)} %all-gather.4.cloned.1.call-done, bf16[256,4096]{0,1:T(8,128)(2,1)} %all-gather.6.cloned.1.call-done), kind=kOutput, calls=%fused_computation.66 | convolution fusion | flops 3221618688 | bytes 15466496 | tf_op jit(solution)/shard_map/dot_general | solution.py:117
  264.7 1.1 copy.35
  265.8 16.2 %all_gather.18 = bf16[1024,256]{0,1:T(8,128)(2,1)S(1)} all-gather(bf16[256,256]{0,1:T(8,128)(2,1)S(1)} %get-tuple-element.604), channel_id=1, replica_groups=mesh['groups'=2,'srv'=4,'hid'=2,'rep'=2] {'srv'}, dimensions={0}, use_global_device_ids=true | all-gather | bytes 655360 | tf_op jit(solution)/shard_map/all_gather | solution.py:125
  282.3 15.0 %all_gather.17 = bf16[1024,256]{0,1:T(8,128)(2,1)S(1)} all-gather(bf16[256,256]{0,1:T(8,128)(2,1)S(1)} %get-tuple-element.605), channel_id=1, replica_groups=mesh['groups'=2,'srv'=4,'hid'=2,'rep'=2] {'srv'}, dimensions={0}, use_global_device_ids=true | all-gather | bytes 655360 | tf_op jit(solution)/shard_map/all_gather | solution.py:124
  297.6 1.0 broadcast_in_dim.55.clone
  298.7 25.6 %while.111 = (s32[]{:T(128)}, bf16[2,128,2,4,128]{4,3,2,1,0:T(4,128)(2,1)}, f32[1024,2,128]{2,0,1:T(8,128)S(1)}, f32[1024,2,128]{2,0,1:T(8,128)}, s32[]{:T(128)}...) while((s32[]{:T(128)}, ...), condition=%wide.region_9.10_spmd, body=%wide.region_0.9_spmd.sunk | while | flops 237806112 | bytes 11565283 | solution.py:148
  298.8 0.8 convert_reduce_fusion.2
  302.3 1.0 constant_dynamic-slice_fusion.2
  303.4 1.0 copy_bitcast_fusion.2
  304.4 0.9 while.112
  305.4 3.1 while.113
  306.1 1.8 fusion.105
  308.7 0.8 constant_dynamic-update-slice_fusion.2
  309.6 0.7 convert_reduce_fusion.2
  313.1 1.0 constant_dynamic-slice_fusion.2
  314.2 1.0 copy_bitcast_fusion.2
  315.2 1.8 while.112
  317.1 6.2 %while.113 = (s32[]{:T(128)}, f32[128,2,4,128]{0,3,2,1:T(8,128)S(1)}, f32[1024,2,128]{2,0,1:T(8,128)S(1)}, f32[1024,2,128]{2,0,1:T(8,128)}, s32[]{:T(128)}, /*in...) while((s32[]{:T(128)}, ...), condition=%wide.region_8.8_spmd.clone, body=%wide.region_7.7_spmd.clone.sunk | while | flops 169197824 | bytes 5222643 | solution.py:99
  317.8 1.8 fusion.105
  320.9 1.8 fusion.105
  322.7 0.3 fusion.103
  323.5 0.8 constant_dynamic-update-slice_fusion.2
  324.3 2.6 copy.41
  327.0 1.3 copy.40
  328.4 0.4 reshape.51
  328.7 48.0 %reduce-scatter.6.cloned.1.call-done = f32[256,2,128]{0,2,1:T(8,128)} async-done(((f32[1024,2,128]{0,2,1:T(8,128)}), f32[256,2,128]{0,2,1:T(8,128)}) %reduce-scatter.6.cloned.1.call-update) | async-done | bytes 262160 | tf_op jit(solution)/shard_map/reduce_scatter | solution.py:155
  376.7 1.0 convert_element_type.44
  377.8 27.5 %reduce-scatter.4.cloned.1.call-done = f32[256,2,128]{0,2,1:T(8,128)} async-done(((f32[1024,2,128]{0,2,1:T(8,128)}), f32[256,2,128]{0,2,1:T(8,128)}) %reduce-scatter.4.cloned.1.call-update) | async-done | bytes 262160 | tf_op jit(solution)/shard_map/reduce_scatter | solution.py:154
  405.2 1.0 convert_element_type.43
  406.3 0.9 pad_maximum_fusion.1
  407.3 14.1 %fusion.44 = f32[256,4096]{1,0:T(8,128)} fusion(bf16[4096,1536]{1,0:T(8,128)(2,1)} %all-gather.4.cloned.1.call-done, bf16[256,256]{1,0:T(8,128)(2,1)S(1)} %copy.43, bf16[256,256]{1,0:T(8,128)(2,1)S(1)} %copy.42, bf16[256,1024]{1,0:T(8,128)(2,1)S(1)} %reshape.51), kind=kOutput, calls=%fused_computation.68 | convolution fusion | flops 3223584768 | bytes 17563648 | tf_op jit(solution)/shard_map/dot_general | solution.py:165
  421.5 92.1 %all_to_all.19 = bf16[256,4,1024]{0,2,1:T(8,128)(2,1)S(1)} all-to-all(bf16[256,4,1024]{0,2,1:T(8,128)(2,1)} %bitcast.213), channel_id=1, replica_groups=mesh['groups'=2,'srv'=4,'hid'=2,'rep'=2] {'srv'}, dimensions={1} | all-to-all | bytes 4194304 | tf_op jit(solution)/shard_map/all_to_all | solution.py:171
  513.6 2.4 copy.44
  515.9 6.4 %convolution_bitcast_fusion.5 = f32[1024,1536]{0,1:T(8,128)S(1)} fusion(bf16[1024,1536]{1,0:T(8,128)(2,1)} %all-gather.8.cloned.1.call-done, bf16[1024,1024]{1,0:T(8,128)(2,1)} %bitcast.214), kind=kOutput, calls=%fused_computation.63 | convolution fusion | flops 3221225472 | bytes 11534336 | tf_op jit(solution)/shard_map/dot_general | solution.py:172
  522.4 2.6 copy-done
  525.0 2.3 slice.37
  527.4 5.4 copy.45
  532.7 1.8 fusion.47
  534.5 1.3 copy.47
  535.8 1.3 copy.46
  537.1 20.0 %reduce-scatter.8.cloned.1.call-done = f32[256,1024]{1,0:T(8,128)} async-done(((f32[256,4096]{1,0:T(8,128)}), f32[256,1024]{1,0:T(8,128)}) %reduce-scatter.8.cloned.1.call-update) | async-done | bytes 1048592 | tf_op jit(solution)/shard_map/reduce_scatter | solution.py:168
  557.1 2.1 convert_element_type.45
  (91 shorter events, 7.9 us)
Async XLA Ops:
  7.2 28.3 %all-gather.6.cloned.1.call-start = ((), (), s32[]{:S(2)}) async-start(), calls=%async_computation.5 | async-start | bytes 2621440 | tf_op jit(solution)/shard_map/all_gather | solution.py:116
  9.3 246.5 %all-gather.4.cloned.1.call-start = ((), (), s32[]{:S(2)}) async-start(), calls=%async_computation.4 | async-start | bytes 15728640 | tf_op jit(solution)/shard_map/all_gather | solution.py:113
  12.5 1.0 copy-start.1
  12.5 364.2 %reduce-scatter.6.cloned.1.call-start = ((), (), s32[]{:S(2)}) async-start(), calls=%async_computation.7 | async-start | bytes 1310720 | tf_op jit(solution)/shard_map/reduce_scatter | solution.py:155
  264.6 34.0 %copy-start.3 = (s32[1024]{0:T(1024)S(1)}, s32[1024]{0:T(1024)}, u32[]{:S(2)}) copy-start(s32[1024]{0:T(1024)} %param.17) | copy-start | bytes 12292
  324.3 4.0 copy-start.2
  326.9 78.3 %reduce-scatter.4.cloned.1.call-start = ((), (), s32[]{:S(2)}) async-start(), calls=%async_computation.6 | async-start | bytes 1310720 | tf_op jit(solution)/shard_map/reduce_scatter | solution.py:154
  328.3 187.6 %all-gather.8.cloned.1.call-start = ((), (), s32[]{:S(2)}) async-start(), calls=%async_computation.9 | async-start | bytes 3932160 | tf_op jit(solution)/shard_map/all_gather | solution.py:174
  407.3 149.8 %reduce-scatter.8.cloned.1.call-start = ((), (), s32[]{:S(2)}) async-start(), calls=%async_computation.8 | async-start | bytes 5242880 | tf_op jit(solution)/shard_map/reduce_scatter | solution.py:168
  522.4 2.7 copy-start
Sparse Core Ops, SparseCore 0:
  10.1 25.2 all-gather.5
  37.6 218.1 all-gather.3
  327.1 49.6 reduce-scatter.5
  379.4 25.7 reduce-scatter.3
  407.4 104.6 all-gather.7
  514.4 42.6 reduce-scatter.7
where the time goes:
time: 567 us; the launch traced here: 566 us
  waiting for transfers between devices  337 us (59%)
  blocking collectives  123 us (22%)
  matrix products  39.3 us (7%)
  local copies, waits for them, and re-layouts  35.5 us (6%)
  between operations  14.2 us (3%)
  other arithmetic  10.7 us (2%)
  loops' own time  6.12 us (1%)
    all_gather x1, waiting for transfers between devices, body(): lax.all_gather(jnp.concatenate([query_weight, key_weight, value_weight],...  220 us
    all_to_all x1, blocking collectives, body(): lax.all_to_all(inputs_all, 'srv', split_axis=1, concat_axis=0, tiled=True)  92.1 us
    reduce_scatter x1, waiting for transfers between devices, body(): lax.psum_scatter(value_accum, 'srv', scatter_dimension=0, tiled=True)  48 us
    reduce_scatter x1, waiting for transfers between devices, body(): lax.psum_scatter(key_accum, 'srv', scatter_dimension=0, tiled=True)  27.5 us
    all_gather x1, waiting for transfers between devices, body(): inputs_all = lax.all_gather(layer_input, ('hid', 'rep'), axis=1, tiled=True)  20.7 us
    reduce_scatter x1, waiting for transfers between devices, body(): lax.psum_scatter(input_terms, ('hid', 'rep'), scatter_dimension=1, tiled=...  20 us
    all_gather x1, blocking collectives, body(): lax.all_gather(values_local, 'srv', axis=0, tiled=True)  16.2 us
    all_gather x1, blocking collectives, body(): lax.all_gather(keys_local, 'srv', axis=0, tiled=True)  15 us
  transfers between devices with their start and end apart: 6, of which 5 were waited for; matrix products, arithmetic and copies ran while one was open for 7% of the time, Pallas kernels for 0%

commit v1 on v0

--- a/solution.py
+++ b/solution.py
@@ -1,6 +1,10 @@
+import functools
+
 import jax
 import jax.numpy as jnp
 from jax import lax
+from jax.experimental import pallas as pl
+from jax.experimental.pallas import tpu as pltpu
 from jax.sharding import PartitionSpec as P
 
 HQ = 32
@@ -183,6 +187,435 @@
     )
 
 
+MESH = pl.DeviceIdType.MESH
+VM = pl.BlockSpec(memory_space=pltpu.VMEM)
+VMEM_BYTES = 60 * 1024 * 1024
+
+
+def place(n_rep):
+    return lax.axis_index("srv"), lax.axis_index("hid") * n_rep + lax.axis_index("rep")
+
+
+def device_at(z, c, n_rep):
+    return {"srv": z, "hid": c // n_rep, "rep": c % n_rep}
+
+
+def greet(n, m, n_rep):
+    z, c = place(n_rep)
+    barrier = pltpu.get_barrier_semaphore()
+    for dz in range(n):
+        for dc in range(m):
+            if dz or dc:
+                pl.semaphore_signal(
+                    barrier,
+                    inc=1,
+                    device_id=device_at((z + dz) % n, (c + dc) % m, n_rep),
+                    device_id_type=MESH,
+                )
+    pl.semaphore_wait(barrier, n * m - 1)
+
+
+def remote(src, dst, send, recv, device):
+    return pltpu.make_async_remote_copy(
+        src_ref=src, dst_ref=dst, send_sem=send, recv_sem=recv, device_id=device, device_id_type=MESH
+    )
+
+
+def rows_at(start, size):
+    return pl.ds(pl.multiple_of(start, size), size)
+
+
+def project_kernel(
+    n, m, n_rep, share,
+    x_ref, og_ref, qw_ref, kw_ref, vw_ref,
+    cols_ref, og_out, qkv_ref,
+    part, took,
+    og_send, og_recv, a_send, a_recv, b_send, b_recv, c_send, c_recv, own_sem,
+):
+    z, c = place(n_rep)
+    tok = x_ref.shape[0]
+    piece = tok // m
+    q_cols = qw_ref.shape[1] // n
+    greet(n, m, n_rep)
+
+    own = c == z
+    for dq in range(m):
+        q = (c + dq) % m
+        src = x_ref.at[rows_at(q * piece, piece)]
+        dst = cols_ref.at[rows_at(z * tok + q * piece, piece)]
+        if dq == 0:
+            @pl.when(own)
+            def _():
+                pltpu.make_async_copy(src, dst, a_recv.at[z]).start()
+
+            @pl.when(jnp.logical_not(own))
+            def _():
+                remote(src, dst, a_send.at[dq], a_recv.at[z], device_at(c, q, n_rep)).start()
+        else:
+            remote(src, dst, a_send.at[dq], a_recv.at[z], device_at(c, q, n_rep)).start()
+    og_dst = og_out.at[rows_at(z * tok, tok)]
+    og_copies = []
+    for d in range(1, n):
+        to = (z + d) % n
+        copy = remote(
+            og_ref.at[:, rows_at(to * q_cols, q_cols)], og_dst,
+            og_send.at[d], og_recv.at[d], device_at(to, c, n_rep),
+        )
+        copy.start()
+        og_copies.append(copy)
+    og_own = pltpu.make_async_copy(og_ref.at[:, rows_at(z * q_cols, q_cols)], og_dst, own_sem)
+    og_own.start()
+
+    def spread_copy(t, d):
+        block = cols_ref.at[rows_at(t * tok + c * piece, piece)]
+        return remote(
+            block, block, b_send.at[t, d], b_recv.at[t, d], device_at(z, (c + d) % m, n_rep)
+        )
+
+    def part_copy(t, d):
+        to = (z + d) % n
+        rows = rows_at(t * tok, tok)
+        return remote(
+            part.at[to, rows], took.at[d - 1, rows],
+            c_send.at[t, d], c_recv.at[t, d], device_at(to, c, n_rep),
+        )
+
+    def spread(i, carry):
+        t = (z + i) % n
+        block = cols_ref.at[rows_at(t * tok + c * piece, piece)]
+        pltpu.make_async_copy(block, block, a_recv.at[t]).wait()
+        for d in range(1, m):
+            spread_copy(t, d).start()
+        return carry
+
+    lax.fori_loop(0, n, spread, 0)
+
+    def multiply(i, carry):
+        t = (z + i) % n
+        for d in range(1, m):
+            spread_copy(t, d).wait_recv()
+        rows = rows_at(t * tok, tok)
+        x = cols_ref[rows, :]
+        keys = jnp.dot(x, kw_ref[...], preferred_element_type=jnp.float32).astype(jnp.bfloat16)
+        values = jnp.dot(x, vw_ref[...], preferred_element_type=jnp.float32).astype(jnp.bfloat16)
+        for s in range(n):
+            j = s // share
+            part[s, rows, :q_cols] = jnp.dot(
+                x, qw_ref[:, s * q_cols : (s + 1) * q_cols], preferred_element_type=jnp.float32
+            ).astype(jnp.bfloat16)
+            part[s, rows, q_cols : q_cols + DH] = keys[:, j * DH : (j + 1) * DH]
+            part[s, rows, q_cols + DH :] = values[:, j * DH : (j + 1) * DH]
+        for d in range(1, n):
+            part_copy(t, d).start()
+        return carry
+
+    lax.fori_loop(0, n, multiply, 0)
+
+    def collect(i, carry):
+        t = (z + i) % n
+        rows = rows_at(t * tok, tok)
+        for d in range(1, n):
+            part_copy(t, d).wait_recv()
+        total = part[z, rows, :].astype(jnp.float32)
+        for d in range(1, n):
+            total = total + took[d - 1, rows, :].astype(jnp.float32)
+        qkv_ref[rows, :] = total.astype(jnp.bfloat16)
+        return carry
+
+    lax.fori_loop(0, n, collect, 0)
+
+    def drain(t, carry):
+        for d in range(1, m):
+            spread_copy(t, d).wait_send()
+        for d in range(1, n):
+            part_copy(t, d).wait_send()
+        return carry
+
+    lax.fori_loop(0, n, drain, 0)
+    og_own.wait()
+    for copy in og_copies:
+        copy.wait()
+    for dq in range(m):
+        q = (c + dq) % m
+        src = x_ref.at[rows_at(q * piece, piece)]
+        dst = cols_ref.at[rows_at(z * tok + q * piece, piece)]
+        copy = remote(src, dst, a_send.at[dq], a_recv.at[z], device_at(c, q, n_rep))
+        if dq == 0:
+            @pl.when(jnp.logical_not(own))
+            def _():
+                copy.wait_send()
+        else:
+            copy.wait_send()
+
+
+def attend_kernel(longest, row_block, qkv_ref, og_ref, dr_ref, dc_ref, dq_ref, mine_ref, give_ref, dk, dv):
+    total_rows = qkv_ref.shape[0]
+    q_cols = og_ref.shape[1]
+    heads = q_cols // DH
+    scale = DH ** (-0.5)
+    dk[...] = jnp.zeros_like(dk)
+    dv[...] = jnp.zeros_like(dv)
+    for first in range(0, total_rows, row_block):
+        last = first + row_block
+        low = max(0, (first + 1 - longest) // 128 * 128)
+        width = last - low
+        queries = jnp.concatenate(
+            [qkv_ref[first:last, h * DH : (h + 1) * DH] for h in range(heads)], axis=0
+        )
+        cotangent = jnp.concatenate(
+            [og_ref[first:last, h * DH : (h + 1) * DH] for h in range(heads)], axis=0
+        )
+        keys = qkv_ref[low:last, q_cols : q_cols + DH]
+        values = qkv_ref[low:last, q_cols + DH :]
+        row_pos = first + lax.broadcasted_iota(jnp.int32, (row_block, width), 0)
+        key_pos = low + lax.broadcasted_iota(jnp.int32, (row_block, width), 1)
+        kept = (dr_ref[first:last, :] == dc_ref[:, low:last]) & (key_pos <= row_pos)
+        allowed = jnp.concatenate([jnp.where(kept, 1.0, 0.0)] * heads, axis=0) > 0.5
+        both = (((1,), (1,)), ((), ()))
+        logits = lax.dot_general(queries, keys, both, preferred_element_type=jnp.float32) * scale
+        logits = jnp.where(allowed, logits, NEGATIVE)
+        weights = jnp.where(allowed, jnp.exp(logits - jnp.max(logits, axis=1, keepdims=True)), 0.0)
+        attention = weights / jnp.sum(weights, axis=1, keepdims=True)
+        slopes = lax.dot_general(cotangent, values, both, preferred_element_type=jnp.float32)
+        inner = jnp.sum(attention * slopes, axis=1, keepdims=True)
+        score_grad = (attention * (slopes - inner) * scale).astype(jnp.bfloat16)
+        down = (((0,), (0,)), ((), ()))
+        query_grad = jnp.dot(score_grad, keys, preferred_element_type=jnp.float32)
+        for h in range(heads):
+            dq_ref[first:last, h * DH : (h + 1) * DH] = query_grad[
+                h * row_block : (h + 1) * row_block
+            ].astype(jnp.bfloat16)
+        dk[low:last, :] += lax.dot_general(
+            score_grad, queries, down, preferred_element_type=jnp.float32
+        )
+        dv[low:last, :] += lax.dot_general(
+            attention.astype(jnp.bfloat16), cotangent, down, preferred_element_type=jnp.float32
+        )
+    odd = lax.axis_index("srv") % 2 == 1
+
+    @pl.when(odd)
+    def _():
+        mine_ref[...] = dv[...]
+        give_ref[...] = dk[...].astype(jnp.bfloat16)
+
+    @pl.when(jnp.logical_not(odd))
+    def _():
+        mine_ref[...] = dk[...]
+        give_ref[...] = dv[...].astype(jnp.bfloat16)
+
+
+def spread_kernel(
+    n, m, n_rep,
+    dq_ref, mine_ref, give_ref, qw_ref, kw_ref, vw_ref,
+    dqa_ref, kva_ref, ig_ref,
+    pair, stage, terms, took, done,
+    p_send, p_recv, q_send, q_recv, k_send, k_recv, r_send, r_recv, e_send, e_recv,
+):
+    z, c = place(n_rep)
+    tok, _ = ig_ref.shape
+    piece = tok // m
+    q_cols = dq_ref.shape[1]
+    greet(n, m, n_rep)
+    odd = z % 2
+    pair_copy = remote(
+        give_ref, pair, p_send, p_recv, device_at(z + 1 - 2 * odd, c, n_rep)
+    )
+    pair_copy.start()
+    my_cols = rows_at(z * q_cols, q_cols)
+    my_head = rows_at((z // 2) * DH, DH)
+
+    def query_copy(t, d):
+        rows = rows_at(t * tok, tok)
+        return remote(
+            dq_ref.at[rows], dqa_ref.at[rows, my_cols],
+            q_send.at[t, d], q_recv.at[t, d], device_at((z + d) % n, c, n_rep),
+        )
+
+    def pair_out(t, d):
+        rows = rows_at(t * tok, tok)
+        return remote(
+            stage.at[rows], kva_ref.at[odd, rows, my_head],
+            k_send.at[t, d], k_recv.at[t, d], device_at((z + d) % n, c, n_rep),
+        )
+
+    def term_copy(t, d):
+        to = (c + d) % m
+        return remote(
+            terms.at[rows_at(t * tok + to * piece, piece)],
+            took.at[d - 1, rows_at(t * piece, piece)],
+            r_send.at[t, d], r_recv.at[t, d], device_at(z, to, n_rep),
+        )
+
+    def done_copy(t):
+        return remote(
+            done.at[rows_at(t * piece, piece)], ig_ref.at[rows_at(c * piece, piece)],
+            e_send.at[t], e_recv.at[c], device_at(t, z, n_rep),
+        )
+
+    for d in range(1, n):
+        query_copy(0, d).start()
+    dqa_ref[:, my_cols] = dq_ref[...]
+    pair_copy.wait()
+    summed = (mine_ref[...] + pair[...].astype(jnp.float32)).astype(jnp.bfloat16)
+    stage[...] = summed
+    kva_ref[odd, :, my_head] = summed
+    for d in range(1, n):
+        pair_out(0, d).start()
+
+    def send_chunk(t, carry):
+        for d in range(1, n):
+            query_copy(t, d).start()
+        for d in range(1, n):
+            pair_out(t, d).start()
+        return carry
+
+    lax.fori_loop(1, n, send_chunk, 0)
+
+    def finish(t):
+        for d in range(1, m):
+            term_copy(t, d).wait_recv()
+        total = terms[rows_at(t * tok + c * piece, piece), :].astype(jnp.float32)
+        for d in range(1, m):
+            total = total + took[d - 1, rows_at(t * piece, piece), :].astype(jnp.float32)
+        done[rows_at(t * piece, piece), :] = total.astype(jnp.bfloat16)
+        own = (t == z) & (c == z)
+
+        @pl.when(own)
+        def _():
+            pltpu.make_async_copy(
+                done.at[rows_at(t * piece, piece)],
+                ig_ref.at[rows_at(c * piece, piece)],
+                e_recv.at[c],
+            ).start()
+
+        @pl.when(jnp.logical_not(own))
+        def _():
+            done_copy(t).start()
+
+    def chunk(t, carry):
+        rows = rows_at(t * tok, tok)
+        for d in range(1, n):
+            query_copy(t, d).wait_recv()
+            pair_out(t, d).wait_recv()
+        across = (((1,), (1,)), ((), ()))
+        total = lax.dot_general(
+            dqa_ref[rows, :], qw_ref[...], across, preferred_element_type=jnp.float32
+        )
+        total = total + lax.dot_general(
+            kva_ref[0, rows, :], kw_ref[...], across, preferred_element_type=jnp.float32
+        )
+        total = total + lax.dot_general(
+            kva_ref[1, rows, :], vw_ref[...], across, preferred_element_type=jnp.float32
+        )
+        terms[rows, :] = total.astype(jnp.bfloat16)
+        for d in range(1, m):
+            term_copy(t, d).start()
+
+        @pl.when(t > 0)
+        def _():
+            finish(t - 1)
+
+        return carry
+
+    lax.fori_loop(0, n, chunk, 0)
+    finish(jnp.int32(n - 1))
+
+    def drain(t, carry):
+        for d in range(1, n):
+            query_copy(t, d).wait_send()
+            pair_out(t, d).wait_send()
+        for d in range(1, m):
+            term_copy(t, d).wait_send()
+
+        @pl.when(jnp.logical_not((t == z) & (c == z)))
+        def _():
+            done_copy(t).wait_send()
+
+        return carry
+
+    lax.fori_loop(0, n, drain, 0)
+    for q in range(m):
+        block = ig_ref.at[q * piece : (q + 1) * piece]
+        pltpu.make_async_copy(block, block, e_recv.at[q]).wait()
+
+
+def stationary(n, n_hid, n_rep, layer_input, query_weight, key_weight, value_weight, out_grad, doc_ids):
+    m = n_hid * n_rep
+    bf16, f32 = jnp.bfloat16, jnp.float32
+    tok, feats = layer_input.shape
+    total = tok * n
+    q_cols = query_weight.shape[1] // n
+    pair_width = key_weight.shape[1]
+    share = n // (pair_width // DH)
+    width = q_cols + 2 * DH
+    dma = pltpu.SemaphoreType.DMA
+    columns, cotangent, qkv = pl.pallas_call(
+        functools.partial(project_kernel, n, m, n_rep, share),
+        out_shape=(
+            jax.ShapeDtypeStruct((total, feats), bf16),
+            jax.ShapeDtypeStruct((total, q_cols), bf16),
+            jax.ShapeDtypeStruct((total, width), bf16),
+        ),
+        in_specs=[VM] * 5,
+        out_specs=(VM,) * 3,
+        scratch_shapes=[
+            pltpu.VMEM((n, total, width), bf16),
+            pltpu.VMEM((n - 1, total, width), bf16),
+            dma((n,)), dma((n,)), dma((m,)), dma((n,)),
+            dma((n, m)), dma((n, m)), dma((n, n)), dma((n, n)), dma,
+        ],
+        compiler_params=pltpu.CompilerParams(
+            collective_id=0, has_side_effects=True, vmem_limit_bytes=VMEM_BYTES
+        ),
+    )(layer_input, out_grad, query_weight, key_weight, value_weight)
+    query_grad, mine, give = pl.pallas_call(
+        functools.partial(attend_kernel, total // 2, BLOCK),
+        out_shape=(
+            jax.ShapeDtypeStruct((total, q_cols), bf16),
+            jax.ShapeDtypeStruct((total, DH), f32),
+            jax.ShapeDtypeStruct((total, DH), bf16),
+        ),
+        in_specs=[VM] * 4,
+        out_specs=(VM,) * 3,
+        scratch_shapes=[pltpu.VMEM((total, DH), f32), pltpu.VMEM((total, DH), f32)],
+        compiler_params=pltpu.CompilerParams(vmem_limit_bytes=VMEM_BYTES),
+    )(qkv, cotangent, doc_ids.reshape(total, 1), doc_ids.reshape(1, total))
+    queries_all, pairs_all, input_grad = pl.pallas_call(
+        functools.partial(spread_kernel, n, m, n_rep),
+        out_shape=(
+            jax.ShapeDtypeStruct((total, q_cols * n), bf16),
+            jax.ShapeDtypeStruct((2, total, pair_width), bf16),
+            jax.ShapeDtypeStruct((tok, feats), bf16),
+        ),
+        in_specs=[VM] * 6,
+        out_specs=(VM,) * 3,
+        scratch_shapes=[
+            pltpu.VMEM((total, DH), bf16),
+            pltpu.VMEM((total, DH), bf16),
+            pltpu.VMEM((total, feats), bf16),
+            pltpu.VMEM((m - 1, tok // m * n, feats), bf16),
+            pltpu.VMEM((tok // m * n, feats), bf16),
+            dma, dma, dma((n, n)), dma((n, n)), dma((n, n)), dma((n, n)),
+            dma((n, m)), dma((n, m)), dma((n,)), dma((m,)),
+        ],
+        compiler_params=pltpu.CompilerParams(
+            collective_id=1, has_side_effects=True, vmem_limit_bytes=VMEM_BYTES
+        ),
+    )(query_grad, mine, give, query_weight, key_weight, value_weight)
+
+    def weight_grad(grads):
+        return lax.dot_general(
+            columns, grads, (((0,), (0,)), ((), ())), preferred_element_type=f32
+        )
+
+    return (
+        input_grad,
+        weight_grad(queries_all),
+        weight_grad(pairs_all[0]),
+        weight_grad(pairs_all[1]),
+    )
+
+
 def solution(mesh):
     in_specs = (
         P(("groups", "srv"), ("hid", "rep")),
@@ -198,4 +631,9 @@
         P(("groups", "srv"), ("hid", "rep")),
         P(("groups", "srv"), ("hid", "rep")),
     )
-    return jax.shard_map(body, mesh=mesh, in_specs=in_specs, out_specs=out_specs, check_vma=False)
+    n, n_hid, n_rep = mesh.shape["srv"], mesh.shape["hid"], mesh.shape["rep"]
+    m = n_hid * n_rep
+    inner = body
+    if n == m and HK % m == 0 and 2 * (HK // m) == n and (HQ // m) % n == 0:
+        inner = functools.partial(stationary, n, n_hid, n_rep)
+    return jax.shard_map(inner, mesh=mesh, in_specs=in_specs, out_specs=out_specs, check_vma=False)

time: 567 us -> 253 us (0.45)
  the two profiles are of different devices: /device:TPU:0 before, /device:TPU:30 now
where the time goes in v1:
time: 253 us
  Pallas kernels  241 us (95%)
  matrix products  9.5 us (4%)
    pallas_call x1, Pallas kernels, stationary(): pl.pallas_call(functools.partial(project_kernel, n, m, n_rep, share), out...  133 us
    pallas_call x1, Pallas kernels, stationary(): pl.pallas_call(functools.partial(spread_kernel, n, m, n_rep), out_shape=(...  99.3 us
    dot_general x3, matrix products, weight_grad(): lax.dot_general(columns, grads, (((0,), (0,)), ((), ())), preferred_eleme...  9.5 us
    pallas_call x1, Pallas kernels, stationary(): pl.pallas_call(functools.partial(attend_kernel, total // 2, BLOCK), out_s...  8.58 us

profile of v1, /device:TPU:30, one launch (start us, length us, event | category | flops | bytes accessed | tf_op | source)
XLA Modules:
  0.0 252.7 jit_solution(16832033983367088625)
XLA Ops:
  0.6 0.0 copy-start.1
  0.6 132.8 %shard_map.93 = (bf16[1024,1024]{1,0:T(8,128)(2,1)}, bf16[1024,256]{1,0:T(8,128)(2,1)}, bf16[1024,512]{1,0:T(8,128)(2,1)}) custom-call(bf16[256,1024]{1,0:T(8,128)(2,1)} %x_ref.1, bf16[256,1024]{1,0:T(8,128)(2,1)} %og_ref.1, bf16[1024,1024]{1,0:T(8,128)(2,1)} %qw_ref.3, bf16[1024,256]{1,0:T(8,128)(2,1)} %kw_ref.3, bf16[1024,256]{1,0:T(8,128)(2,1)} %vw_ref.3), custom_call_target="tpu_custom_call" | custom-call | tf_op jit(solution)/shard_map/pallas_call | solution.py:552
  133.4 0.0 copy-done.1
  133.5 1.0 copy.10.dr_ref
  134.5 8.6 %shard_map.94 = (bf16[1024,256]{1,0:T(8,128)(2,1)}, f32[1024,128]{1,0:T(8,128)}, bf16[1024,128]{1,0:T(8,128)(2,1)}) custom-call(bf16[1024,512]{1,0:T(8,128)(2,1)} %get-tuple-element.13.qkv_ref, bf16[1024,256]{1,0:T(8,128)(2,1)} %get-tuple-element.14.og_ref, s32[1024,1]{1,0:T(8,128)} %copy.10.dr_ref, s32[1,1024]{1,0:T(1,128)} %bitcast.12), custom_call_target="tpu_custom_call" | custom-call | tf_op jit(solution)/shard_map/pallas_call | solution.py:571
  143.1 0.0 copy-start.2
  143.1 99.3 %shard_map.95 = (bf16[1024,1024]{1,0:T(8,128)(2,1)}, bf16[2,1024,256]{2,1,0:T(8,128)(2,1)}, bf16[256,1024]{1,0:T(8,128)(2,1)}) custom-call(bf16[1024,256]{1,0:T(8,128)(2,1)} %get-tuple-element.15.dq_ref, f32[1024,128]{1,0:T(8,128)} %get-tuple-element.16.mine_ref, bf16[1024,128]{1,0:T(8,128)(2,1)} %get-tuple-element.17.give_ref, bf16[1024,1024]{1,0:T(8,128)(2,1)} %qw_ref.3, ...), custom_call_target="tpu_custom_call" | custom-call | tf_op jit(solution)/shard_map/pallas_call | solution.py:583
  242.4 0.0 copy-done.2
  242.4 0.0 copy-start.3
  242.4 6.1 %fusion.6 = f32[1024,1024]{1,0:T(8,128)} fusion(bf16[1024,1024]{1,0:T(8,128)(2,1)S(1)} %copy-done.2, bf16[1024,1024]{1,0:T(8,128)(2,1)} %get-tuple-element.20), kind=kOutput, calls=%fused_computation.6 | convolution fusion | flops 2147483648 | bytes 8388608 | tf_op jit(solution)/shard_map/dot_general | solution.py:607
  248.5 0.0 copy-done.3
  248.5 1.7 fusion.2
  250.2 0.0 copy-start
  250.2 1.7 fusion
  251.9 0.0 copy-done
  251.9 0.8 copy.12
Async XLA Ops:
  0.6 132.8 %copy-start.1 = (s32[1024]{0:T(1024)S(1)}, s32[1024]{0:T(1024)}, u32[]{:S(2)}) copy-start(s32[1024]{0:T(1024)} %param.11) | copy-start | bytes 12292
  143.1 99.3 %copy-start.2 = (bf16[1024,1024]{1,0:T(8,128)(2,1)S(1)}, bf16[1024,1024]{1,0:T(8,128)(2,1)}, u32[]{:S(2)}) copy-start(bf16[1024,1024]{1,0:T(8,128)(2,1)} %get-tuple-element.19) | copy-start | bytes 6291460
  242.4 6.1 %copy-start.3 = (bf16[2,1024,256]{2,1,0:T(8,128)(2,1)S(1)}, bf16[2,1024,256]{2,1,0:T(8,128)(2,1)}, u32[]{:S(2)}) copy-start(bf16[2,1024,256]{2,1,0:T(8,128)(2,1)} %get-tuple-element.21) | copy-start | bytes 3145732
  250.2 1.7 copy-start

commit v2 on v1

--- a/solution.py
+++ b/solution.py
@@ -229,13 +229,18 @@
     n, m, n_rep, share,
     x_ref, og_ref, qw_ref, kw_ref, vw_ref,
     cols_ref, og_out, qkv_ref,
-    part, took,
-    og_send, og_recv, a_send, a_recv, b_send, b_recv, c_send, c_recv, own_sem,
+    part, took, relay,
+    og_send, og_recv, a_send, a_recv, b_send, b_recv, c_send, c_recv, v_send, v_recv, own_sem,
 ):
     z, c = place(n_rep)
     tok = x_ref.shape[0]
     piece = tok // m
     q_cols = qw_ref.shape[1] // n
+    half, odd = z // 2, z % 2
+    partner = z + 1 - 2 * odd
+    middle = half != odd
+    far = 2 * (1 - half)
+    kv_cols = rows_at(q_cols + odd * DH, DH)
     greet(n, m, n_rep)
 
     own = c == z
@@ -272,16 +277,41 @@
             block, block, b_send.at[t, d], b_recv.at[t, d], device_at(z, (c + d) % m, n_rep)
         )
 
-    def part_copy(t, d):
-        to = (z + d) % n
-        rows = rows_at(t * tok, tok)
+    def part_copy(t, slot):
+        rows = rows_at(t * tok, tok)
+        src = part.at[partner if slot == 0 else far + slot - 1, rows]
+        dst = took.at[0, rows] if slot == 0 else relay.at[slot - 1, rows]
         return remote(
-            part.at[to, rows], took.at[d - 1, rows],
-            c_send.at[t, d], c_recv.at[t, d], device_at(to, c, n_rep),
-        )
+            src, dst, c_send.at[t, slot], c_recv.at[t, slot], device_at(partner, c, n_rep)
+        )
+
+    def far_copy(t, slot):
+        to = far + slot - 1
+        rows = rows_at(t * tok, tok)
+        return remote(
+            part.at[to, rows], took.at[1, rows],
+            c_send.at[t, slot], c_recv.at[t, 3], device_at(to, c, n_rep),
+        )
+
+    def swap_copy(t):
+        block = qkv_ref.at[rows_at(t * tok, tok), kv_cols]
+        return remote(block, block, v_send.at[t], v_recv.at[t], device_at(partner, c, n_rep))
+
+    def pass_on(t):
+        rows = rows_at(t * tok, tok)
+
+        @pl.when(middle)
+        def _():
+            for slot in (1, 2):
+                part_copy(t, slot).wait_recv()
+                to = far + slot - 1
+                total = part[to, rows, :].astype(jnp.float32)
+                total = total + relay[slot - 1, rows, :].astype(jnp.float32)
+                part[to, rows, :] = total.astype(jnp.bfloat16)
+                far_copy(t, slot).start()
 
     def spread(i, carry):
-        t = (z + i) % n
+        t = (2 * half + i) % n
         block = cols_ref.at[rows_at(t * tok + c * piece, piece)]
         pltpu.make_async_copy(block, block, a_recv.at[t]).wait()
         for d in range(1, m):
@@ -291,7 +321,7 @@
     lax.fori_loop(0, n, spread, 0)
 
     def multiply(i, carry):
-        t = (z + i) % n
+        t = (2 * half + i) % n
         for d in range(1, m):
             spread_copy(t, d).wait_recv()
         rows = rows_at(t * tok, tok)
@@ -303,23 +333,37 @@
             part[s, rows, :q_cols] = jnp.dot(
                 x, qw_ref[:, s * q_cols : (s + 1) * q_cols], preferred_element_type=jnp.float32
             ).astype(jnp.bfloat16)
-            part[s, rows, q_cols : q_cols + DH] = keys[:, j * DH : (j + 1) * DH]
-            part[s, rows, q_cols + DH :] = values[:, j * DH : (j + 1) * DH]
-        for d in range(1, n):
-            part_copy(t, d).start()
+            pair = values if s % 2 else keys
+            part[s, rows, q_cols:] = pair[:, j * DH : (j + 1) * DH]
+
+        @pl.when(jnp.logical_not(middle))
+        def _():
+            for slot in (1, 2):
+                part_copy(t, slot).start()
+
+        part_copy(t, 0).start()
+
+        @pl.when(i > 0)
+        def _():
+            pass_on((2 * half + i - 1) % n)
+
         return carry
 
     lax.fori_loop(0, n, multiply, 0)
+    pass_on((2 * half + n - 1) % n)
 
     def collect(i, carry):
-        t = (z + i) % n
-        rows = rows_at(t * tok, tok)
-        for d in range(1, n):
-            part_copy(t, d).wait_recv()
+        t = (2 * half + i) % n
+        rows = rows_at(t * tok, tok)
+        part_copy(t, 0).wait_recv()
+        pltpu.make_async_copy(took.at[1, rows], took.at[1, rows], c_recv.at[t, 3]).wait()
         total = part[z, rows, :].astype(jnp.float32)
-        for d in range(1, n):
-            total = total + took[d - 1, rows, :].astype(jnp.float32)
-        qkv_ref[rows, :] = total.astype(jnp.bfloat16)
+        for slot in range(2):
+            total = total + took[slot, rows, :].astype(jnp.float32)
+        total = total.astype(jnp.bfloat16)
+        qkv_ref[rows, :q_cols] = total[:, :q_cols]
+        qkv_ref[rows, kv_cols] = total[:, q_cols:]
+        swap_copy(t).start()
         return carry
 
     lax.fori_loop(0, n, collect, 0)
@@ -327,8 +371,9 @@
     def drain(t, carry):
         for d in range(1, m):
             spread_copy(t, d).wait_send()
-        for d in range(1, n):
-            part_copy(t, d).wait_send()
+        for slot in range(3):
+            part_copy(t, slot).wait_send()
+        swap_copy(t).wait()
         return carry
 
     lax.fori_loop(0, n, drain, 0)
@@ -416,27 +461,45 @@
     piece = tok // m
     q_cols = dq_ref.shape[1]
     greet(n, m, n_rep)
-    odd = z % 2
-    pair_copy = remote(
-        give_ref, pair, p_send, p_recv, device_at(z + 1 - 2 * odd, c, n_rep)
-    )
+    half, odd = z // 2, z % 2
+    partner = z + 1 - 2 * odd
+    middle = half != odd
+    far = 2 * (1 - half)
+    near = 2 - half
+    pair_copy = remote(give_ref, pair, p_send, p_recv, device_at(partner, c, n_rep))
     pair_copy.start()
     my_cols = rows_at(z * q_cols, q_cols)
-    my_head = rows_at((z // 2) * DH, DH)
-
-    def query_copy(t, d):
-        rows = rows_at(t * tok, tok)
+    my_head = rows_at(half * DH, DH)
+
+    def query_copy(t, slot):
+        rows = rows_at(t * tok, tok)
+        owner = z if slot < 2 else far + slot - 2
+        there = dqa_ref.at[rows, rows_at(owner * q_cols, q_cols)]
         return remote(
-            dq_ref.at[rows], dqa_ref.at[rows, my_cols],
-            q_send.at[t, d], q_recv.at[t, d], device_at((z + d) % n, c, n_rep),
-        )
-
-    def pair_out(t, d):
-        rows = rows_at(t * tok, tok)
+            dq_ref.at[rows] if slot < 2 else there, there,
+            q_send.at[t, slot], q_recv.at[t, owner],
+            device_at(near if slot == 1 else partner, c, n_rep),
+        )
+
+    def pair_out(t, slot):
+        rows = rows_at(t * tok, tok)
+        owner = z if slot < 2 else far + slot - 2
+        there = kva_ref.at[owner % 2, rows, rows_at(owner // 2 * DH, DH)]
         return remote(
-            stage.at[rows], kva_ref.at[odd, rows, my_head],
-            k_send.at[t, d], k_recv.at[t, d], device_at((z + d) % n, c, n_rep),
-        )
+            stage.at[rows] if slot < 2 else there, there,
+            k_send.at[t, slot], k_recv.at[t, owner],
+            device_at(near if slot == 1 else partner, c, n_rep),
+        )
+
+    def await_owner(t, owner):
+        rows = rows_at(t * tok, tok)
+        block = dqa_ref.at[rows, rows_at(owner * q_cols, q_cols)]
+        pltpu.make_async_copy(block, block, q_recv.at[t, owner]).wait()
+
+    def await_pair(t, owner):
+        rows = rows_at(t * tok, tok)
+        block = kva_ref.at[owner % 2, rows, rows_at(owner // 2 * DH, DH)]
+        pltpu.make_async_copy(block, block, k_recv.at[t, owner]).wait()
 
     def term_copy(t, d):
         to = (c + d) % m
@@ -452,21 +515,20 @@
             e_send.at[t], e_recv.at[c], device_at(t, z, n_rep),
         )
 
-    for d in range(1, n):
-        query_copy(0, d).start()
+    for slot in (1, 0):
+        query_copy(0, slot).start()
     dqa_ref[:, my_cols] = dq_ref[...]
     pair_copy.wait()
     summed = (mine_ref[...] + pair[...].astype(jnp.float32)).astype(jnp.bfloat16)
     stage[...] = summed
     kva_ref[odd, :, my_head] = summed
-    for d in range(1, n):
-        pair_out(0, d).start()
+    for slot in (1, 0):
+        pair_out(0, slot).start()
 
     def send_chunk(t, carry):
-        for d in range(1, n):
-            query_copy(t, d).start()
-        for d in range(1, n):
-            pair_out(t, d).start()
+        for slot in (1, 0):
+            query_copy(t, slot).start()
+            pair_out(t, slot).start()
         return carry
 
     lax.fori_loop(1, n, send_chunk, 0)
@@ -494,9 +556,22 @@
 
     def chunk(t, carry):
         rows = rows_at(t * tok, tok)
-        for d in range(1, n):
-            query_copy(t, d).wait_recv()
-            pair_out(t, d).wait_recv()
+        for slot in (2, 3):
+            await_owner(t, far + slot - 2)
+
+            @pl.when(middle)
+            def _():
+                query_copy(t, slot).start()
+
+        for slot in (2, 3):
+            await_pair(t, far + slot - 2)
+
+            @pl.when(middle)
+            def _():
+                pair_out(t, slot).start()
+
+        await_owner(t, partner)
+        await_pair(t, partner)
         across = (((1,), (1,)), ((), ()))
         total = lax.dot_general(
             dqa_ref[rows, :], qw_ref[...], across, preferred_element_type=jnp.float32
@@ -521,9 +596,16 @@
     finish(jnp.int32(n - 1))
 
     def drain(t, carry):
-        for d in range(1, n):
-            query_copy(t, d).wait_send()
-            pair_out(t, d).wait_send()
+        for slot in (0, 1):
+            query_copy(t, slot).wait_send()
+            pair_out(t, slot).wait_send()
+
+        @pl.when(middle)
+        def _():
+            for slot in (2, 3):
+                query_copy(t, slot).wait_send()
+                pair_out(t, slot).wait_send()
+
         for d in range(1, m):
             term_copy(t, d).wait_send()
 
@@ -559,10 +641,11 @@
         in_specs=[VM] * 5,
         out_specs=(VM,) * 3,
         scratch_shapes=[
-            pltpu.VMEM((n, total, width), bf16),
-            pltpu.VMEM((n - 1, total, width), bf16),
+            pltpu.VMEM((n, total, q_cols + DH), bf16),
+            pltpu.VMEM((2, total, q_cols + DH), bf16),
+            pltpu.VMEM((2, total, q_cols + DH), bf16),
             dma((n,)), dma((n,)), dma((m,)), dma((n,)),
-            dma((n, m)), dma((n, m)), dma((n, n)), dma((n, n)), dma,
+            dma((n, m)), dma((n, m)), dma((n, 3)), dma((n, 4)), dma((n,)), dma((n,)), dma,
         ],
         compiler_params=pltpu.CompilerParams(
             collective_id=0, has_side_effects=True, vmem_limit_bytes=VMEM_BYTES

time: 253 us -> 203 us (0.80)
  the two profiles are of different devices: /device:TPU:30 before, /device:TPU:0 now
where the time goes in v2:
time: 203 us; the launch traced here: 202 us
  Pallas kernels  190 us (94%)
  matrix products  9.5 us (5%)
    pallas_call x1, Pallas kernels, stationary(): pl.pallas_call(functools.partial(project_kernel, n, m, n_rep, share), out...  94.1 us
    pallas_call x1, Pallas kernels, stationary(): pl.pallas_call(functools.partial(spread_kernel, n, m, n_rep), out_shape=(...  87.5 us
    dot_general x3, matrix products, weight_grad(): lax.dot_general(columns, grads, (((0,), (0,)), ((), ())), preferred_eleme...  9.5 us
    pallas_call x1, Pallas kernels, stationary(): pl.pallas_call(functools.partial(attend_kernel, total // 2, BLOCK), out_s...  8.6 us

profile of v2, /device:TPU:0, one launch (start us, length us, event | category | flops | bytes accessed | tf_op | source)
XLA Modules:
  0.0 202.3 jit_solution(7425564315647580804)
XLA Ops:
  0.6 0.0 copy-start.1
  0.6 94.1 %shard_map.93 = (bf16[1024,1024]{1,0:T(8,128)(2,1)}, bf16[1024,256]{1,0:T(8,128)(2,1)}, bf16[1024,512]{1,0:T(8,128)(2,1)}) custom-call(bf16[256,1024]{1,0:T(8,128)(2,1)} %x_ref.1, bf16[256,1024]{1,0:T(8,128)(2,1)} %og_ref.1, bf16[1024,1024]{1,0:T(8,128)(2,1)} %qw_ref.3, bf16[1024,256]{1,0:T(8,128)(2,1)} %kw_ref.3, bf16[1024,256]{1,0:T(8,128)(2,1)} %vw_ref.3), custom_call_target="tpu_custom_call" | custom-call | tf_op jit(solution)/shard_map/pallas_call | solution.py:634
  94.8 0.0 copy-done.1
  94.8 1.0 copy.10.dr_ref
  95.8 8.6 %shard_map.94 = (bf16[1024,256]{1,0:T(8,128)(2,1)}, f32[1024,128]{1,0:T(8,128)}, bf16[1024,128]{1,0:T(8,128)(2,1)}) custom-call(bf16[1024,512]{1,0:T(8,128)(2,1)} %get-tuple-element.13.qkv_ref, bf16[1024,256]{1,0:T(8,128)(2,1)} %get-tuple-element.14.og_ref, s32[1024,1]{1,0:T(8,128)} %copy.10.dr_ref, s32[1,1024]{1,0:T(1,128)} %bitcast.12), custom_call_target="tpu_custom_call" | custom-call | tf_op jit(solution)/shard_map/pallas_call | solution.py:654
  104.4 0.0 copy-start.2
  104.4 87.5 %shard_map.95 = (bf16[1024,1024]{1,0:T(8,128)(2,1)}, bf16[2,1024,256]{2,1,0:T(8,128)(2,1)}, bf16[256,1024]{1,0:T(8,128)(2,1)}) custom-call(bf16[1024,256]{1,0:T(8,128)(2,1)} %get-tuple-element.15.dq_ref, f32[1024,128]{1,0:T(8,128)} %get-tuple-element.16.mine_ref, bf16[1024,128]{1,0:T(8,128)(2,1)} %get-tuple-element.17.give_ref, bf16[1024,1024]{1,0:T(8,128)(2,1)} %qw_ref.3, ...), custom_call_target="tpu_custom_call" | custom-call | tf_op jit(solution)/shard_map/pallas_call | solution.py:666
  191.9 0.0 copy-done.2
  191.9 0.0 copy-start.3
  191.9 6.1 %fusion.6 = f32[1024,1024]{1,0:T(8,128)} fusion(bf16[1024,1024]{1,0:T(8,128)(2,1)S(1)} %copy-done.2, bf16[1024,1024]{1,0:T(8,128)(2,1)} %get-tuple-element.20), kind=kOutput, calls=%fused_computation.6 | convolution fusion | flops 2147483648 | bytes 8388608 | tf_op jit(solution)/shard_map/dot_general | solution.py:690
  198.0 0.0 copy-done.3
  198.0 1.7 fusion.2
  199.7 0.0 copy-start
  199.7 1.7 fusion
  201.5 0.0 copy-done
  201.5 0.8 copy.12
Async XLA Ops:
  0.6 94.1 %copy-start.1 = (s32[1024]{0:T(1024)S(1)}, s32[1024]{0:T(1024)}, u32[]{:S(2)}) copy-start(s32[1024]{0:T(1024)} %param.11) | copy-start | bytes 12292
  104.4 87.5 %copy-start.2 = (bf16[1024,1024]{1,0:T(8,128)(2,1)S(1)}, bf16[1024,1024]{1,0:T(8,128)(2,1)}, u32[]{:S(2)}) copy-start(bf16[1024,1024]{1,0:T(8,128)(2,1)} %get-tuple-element.19) | copy-start | bytes 6291460
  191.9 6.1 %copy-start.3 = (bf16[2,1024,256]{2,1,0:T(8,128)(2,1)S(1)}, bf16[2,1024,256]{2,1,0:T(8,128)(2,1)}, u32[]{:S(2)}) copy-start(bf16[2,1024,256]{2,1,0:T(8,128)(2,1)} %get-tuple-element.21) | copy-start | bytes 3145732
  199.7 1.7 copy-start

commit v3 on v2

--- a/solution.py
+++ b/solution.py
@@ -516,16 +516,17 @@
         )
 
     for slot in (1, 0):
-        query_copy(0, slot).start()
+        query_copy(n - 1, slot).start()
     dqa_ref[:, my_cols] = dq_ref[...]
     pair_copy.wait()
     summed = (mine_ref[...] + pair[...].astype(jnp.float32)).astype(jnp.bfloat16)
     stage[...] = summed
     kva_ref[odd, :, my_head] = summed
     for slot in (1, 0):
-        pair_out(0, slot).start()
-
-    def send_chunk(t, carry):
+        pair_out(n - 1, slot).start()
+
+    def send_chunk(i, carry):
+        t = (i + n - 1) % n
         for slot in (1, 0):
             query_copy(t, slot).start()
             pair_out(t, slot).start()
@@ -554,7 +555,8 @@
         def _():
             done_copy(t).start()
 
-    def chunk(t, carry):
+    def chunk(i, carry):
+        t = (i + n - 1) % n
         rows = rows_at(t * tok, tok)
         for slot in (2, 3):
             await_owner(t, far + slot - 2)
@@ -586,14 +588,14 @@
         for d in range(1, m):
             term_copy(t, d).start()
 
-        @pl.when(t > 0)
+        @pl.when(i > 0)
         def _():
-            finish(t - 1)
+            finish((i + n - 2) % n)
 
         return carry
 
     lax.fori_loop(0, n, chunk, 0)
-    finish(jnp.int32(n - 1))
+    finish(jnp.int32(n - 2))
 
     def drain(t, carry):
         for slot in (0, 1):

time: 203 us -> 203 us (level)
  no operation moved by 1% of the time
where the time goes in v3:
time: 203 us; the launch traced here: 202 us
  Pallas kernels  190 us (94%)
  matrix products  9.5 us (5%)
    pallas_call x1, Pallas kernels, stationary(): pl.pallas_call(functools.partial(project_kernel, n, m, n_rep, share), out...  94.1 us
    pallas_call x1, Pallas kernels, stationary(): pl.pallas_call(functools.partial(spread_kernel, n, m, n_rep), out_shape=(...  87.5 us
    dot_general x3, matrix products, weight_grad(): lax.dot_general(columns, grads, (((0,), (0,)), ((), ())), preferred_eleme...  9.5 us
    pallas_call x1, Pallas kernels, stationary(): pl.pallas_call(functools.partial(attend_kernel, total // 2, BLOCK), out_s...  8.6 us

profile of v3, /device:TPU:0, one launch (start us, length us, event | category | flops | bytes accessed | tf_op | source)
XLA Modules:
  0.0 202.2 jit_solution(10460954362382568891)
XLA Ops:
  0.6 0.0 copy-start.1
  0.6 94.1 %shard_map.93 = (bf16[1024,1024]{1,0:T(8,128)(2,1)}, bf16[1024,256]{1,0:T(8,128)(2,1)}, bf16[1024,512]{1,0:T(8,128)(2,1)}) custom-call(bf16[256,1024]{1,0:T(8,128)(2,1)} %x_ref.1, bf16[256,1024]{1,0:T(8,128)(2,1)} %og_ref.1, bf16[1024,1024]{1,0:T(8,128)(2,1)} %qw_ref.3, bf16[1024,256]{1,0:T(8,128)(2,1)} %kw_ref.3, bf16[1024,256]{1,0:T(8,128)(2,1)} %vw_ref.3), custom_call_target="tpu_custom_call" | custom-call | tf_op jit(solution)/shard_map/pallas_call | solution.py:636
  94.8 0.0 copy-done.1
  94.8 1.0 copy.10.dr_ref
  95.8 8.6 %shard_map.94 = (bf16[1024,256]{1,0:T(8,128)(2,1)}, f32[1024,128]{1,0:T(8,128)}, bf16[1024,128]{1,0:T(8,128)(2,1)}) custom-call(bf16[1024,512]{1,0:T(8,128)(2,1)} %get-tuple-element.13.qkv_ref, bf16[1024,256]{1,0:T(8,128)(2,1)} %get-tuple-element.14.og_ref, s32[1024,1]{1,0:T(8,128)} %copy.10.dr_ref, s32[1,1024]{1,0:T(1,128)} %bitcast.12), custom_call_target="tpu_custom_call" | custom-call | tf_op jit(solution)/shard_map/pallas_call | solution.py:656
  104.4 0.0 copy-start.2
  104.4 87.5 %shard_map.95 = (bf16[1024,1024]{1,0:T(8,128)(2,1)}, bf16[2,1024,256]{2,1,0:T(8,128)(2,1)}, bf16[256,1024]{1,0:T(8,128)(2,1)}) custom-call(bf16[1024,256]{1,0:T(8,128)(2,1)} %get-tuple-element.15.dq_ref, f32[1024,128]{1,0:T(8,128)} %get-tuple-element.16.mine_ref, bf16[1024,128]{1,0:T(8,128)(2,1)} %get-tuple-element.17.give_ref, bf16[1024,1024]{1,0:T(8,128)(2,1)} %qw_ref.3, ...), custom_call_target="tpu_custom_call" | custom-call | tf_op jit(solution)/shard_map/pallas_call | solution.py:668
  191.9 0.0 copy-done.2
  191.9 0.0 copy-start.3
  191.9 6.1 %fusion.6 = f32[1024,1024]{1,0:T(8,128)} fusion(bf16[1024,1024]{1,0:T(8,128)(2,1)S(1)} %copy-done.2, bf16[1024,1024]{1,0:T(8,128)(2,1)} %get-tuple-element.20), kind=kOutput, calls=%fused_computation.6 | convolution fusion | flops 2147483648 | bytes 8388608 | tf_op jit(solution)/shard_map/dot_general | solution.py:692
  198.0 0.0 copy-done.3
  198.0 1.7 fusion.2
  199.7 0.0 copy-start
  199.7 1.7 fusion
  201.4 0.0 copy-done
  201.4 0.8 copy.12
Async XLA Ops:
  0.6 94.1 %copy-start.1 = (s32[1024]{0:T(1024)S(1)}, s32[1024]{0:T(1024)}, u32[]{:S(2)}) copy-start(s32[1024]{0:T(1024)} %param.11) | copy-start | bytes 12292
  104.4 87.5 %copy-start.2 = (bf16[1024,1024]{1,0:T(8,128)(2,1)S(1)}, bf16[1024,1024]{1,0:T(8,128)(2,1)}, u32[]{:S(2)}) copy-start(bf16[1024,1024]{1,0:T(8,128)(2,1)} %get-tuple-element.19) | copy-start | bytes 6291460
  191.9 6.1 %copy-start.3 = (bf16[2,1024,256]{2,1,0:T(8,128)(2,1)S(1)}, bf16[2,1024,256]{2,1,0:T(8,128)(2,1)}, u32[]{:S(2)}) copy-start(bf16[2,1024,256]{2,1,0:T(8,128)(2,1)} %get-tuple-element.21) | copy-start | bytes 3145732
  199.7 1.7 copy-start
